TPU v7x, 512 devices: a whole 4x8x8 slice. The times are simulated.
512 devices in a mesh: dp: 32 (over z, x_hi, core), fsdp: 16 (over x_lo, y).
Axes of the slice: x: 4 (x_hi: 2, x_lo: 2; x = x_hi * 2 + x_lo), y: 8, z: 8, core: 2. Of those that a mesh axis runs over, the one named last changes fastest.
Arguments:
- activations: bfloat16 [98304, 4096], P(('dp', 'fsdp')), may hold values from -24 to 24
- cotangent: bfloat16 [98304, 512], P(('dp', 'fsdp')), may hold values from -6 to 6
- weight: bfloat16 [4096, 512], P('fsdp'), may hold values from -0.09375 to 0.09375
- momentum: float32 [32, 4096, 512], P('dp', 'fsdp'), may hold values from -256 to 256
- positions: int32 [16, 32, 512], P('fsdp'), may hold values from 0 to 255, as said below
Outputs:
- grad_input: bfloat16 [98304, 4096], P(('dp', 'fsdp'))
- new_momentum: float32 [32, 4096, 512], P('dp', 'fsdp')
- update: bfloat16 [4096, 512], P('fsdp')
Inputs may be any that keep to these rules, and one draw needn't show every extreme that they name: For each block b and column c the 32 values positions[b, :, c] are distinct.
All inputs are finite; a program needn't handle non-finite values.
Results may differ from a plain program's by a relative error of at most 0.023.
Values may be sent and summed in bfloat16 or wider, within the bound.
A program may use at most 64 MiB of HBM per device.

v0:
```python
import math
import jax
import jax.numpy as jnp
from jax import lax
from jax.sharding import PartitionSpec as P

SPAN = 256
MOMENTUM_DECAY = 0.999


def transform_table(length):
    freq = jnp.arange(length, dtype=jnp.float32)[:, None]
    place = jnp.arange(length, dtype=jnp.float32)[None, :]
    angles = jnp.pi * (2.0 * place + 1.0) * freq / (2.0 * length)
    scales = jnp.where(freq == 0.0, jnp.sqrt(1.0 / length), jnp.sqrt(2.0 / length))
    return scales * jnp.cos(angles)


def forward_blocks(table, blocks):
    return jnp.einsum("kn,bnc->bkc", table, blocks, precision=lax.Precision.HIGHEST)


def inverse_blocks(table, coeffs):
    return jnp.einsum("kn,bkc->bnc", table, coeffs, precision=lax.Precision.HIGHEST)


def grouped_positions(positions):
    blocks, picks, columns = positions.shape
    group = math.gcd(picks, 8)
    stacked = positions.reshape(blocks, picks // group, group, columns)
    return (jnp.transpose(stacked, (1, 0, 2, 3)), group)


def pick_band(coeffs, positions):
    blocks, length, columns = coeffs.shape
    picks = positions.shape[1]
    stacked, group = grouped_positions(positions)
    levels = jnp.arange(length, dtype=jnp.int32)[None, None, :, None]

    def one_group(where):
        onehot = where[:, :, None, :] == levels
        return jnp.sum(jnp.where(onehot, coeffs[:, None, :, :], 0.0), axis=2)

    found = lax.map(one_group, stacked)
    return jnp.transpose(found, (1, 0, 2, 3)).reshape(blocks, picks, columns)


def place_band(values, positions, length):
    blocks, picks, columns = values.shape
    stacked, group = grouped_positions(positions)
    stacked_values = jnp.transpose(
        values.reshape(blocks, picks // group, group, columns), (1, 0, 2, 3)
    )
    levels = jnp.arange(length, dtype=jnp.int32)[None, None, :, None]

    def add_group(dense, packed):
        where, amounts = packed
        onehot = where[:, :, None, :] == levels
        return (dense + jnp.sum(jnp.where(onehot, amounts[:, :, None, :], 0.0), axis=1), None)

    start = jnp.zeros((blocks, length, columns), jnp.float32)
    dense, unused = lax.scan(add_group, start, (stacked, stacked_values))
    return dense


def contract_last(left, right):
    return lax.dot_general(
        left, right, (((1,), (1,)), ((), ())), preferred_element_type=jnp.float32
    )


def on_device(activations, cotangent, weight, momentum, positions):
    table = transform_table(SPAN)
    grad_input = contract_last(
        cotangent, lax.all_gather(weight, "fsdp", axis=0, tiled=True)
    ).astype(jnp.bfloat16)
    gradient = lax.psum_scatter(
        lax.dot_general(
            activations, cotangent, (((0,), (0,)), ((), ())), preferred_element_type=jnp.float32
        ).astype(jnp.bfloat16),
        "fsdp",
        scatter_dimension=0,
        tiled=True,
    ).astype(jnp.float32)
    moment = MOMENTUM_DECAY * momentum[0] + gradient
    blocks = moment.reshape(positions.shape[0], SPAN, moment.shape[1])
    coeffs = forward_blocks(table, blocks)
    picked = pick_band(coeffs, positions)
    kept = blocks - inverse_blocks(table, place_band(picked, positions, SPAN))
    new_momentum = kept.reshape(moment.shape)[None]
    bands = picked.astype(jnp.bfloat16)
    replicas = lax.axis_size("dp")
    summed = jnp.sum(
        lax.all_gather(bands[None], "dp", axis=0, tiled=True).astype(jnp.float32), axis=0
    )
    mean_band = summed / replicas
    update = (
        inverse_blocks(table, place_band(mean_band, positions, SPAN))
        .reshape(moment.shape)
        .astype(jnp.bfloat16)
    )
    return (grad_input, new_momentum, update)


def solution(mesh):
    placed = (
        P(("dp", "fsdp"), None),
        P(("dp", "fsdp"), None),
        P("fsdp", None),
        P("dp", "fsdp", None),
        P("fsdp", None, None),
    )
    return jax.shard_map(
        on_device,
        mesh=mesh,
        in_specs=placed,
        out_specs=(P(("dp", "fsdp"), None), P("dp", "fsdp", None), P("fsdp", None)),
        check_vma=False,
    )
```

profile of v0, /device:TPU:1, one launch (start us, length us, event | category | flops | bytes accessed | tf_op | source)
XLA Modules:
  0.0 280.2 jit_solution(7000928409608363338)
XLA Ops:
  7.2 0.0 copy-start
  7.2 0.0 all-gather.3.cloned.1.call-start
  7.2 0.7 all-gather.3.cloned.1.call-update
  7.9 0.0 reduce-scatter.2.cloned.1.call-start
  8.0 0.6 copy-done
  8.6 4.2 %convolution_convert_fusion = bf16[4096,512]{1,0:T(8,128)(2,1)} fusion(bf16[192,4096]{1,0:T(8,128)(2,1)S(1)} %copy-done, bf16[192,512]{1,0:T(8,128)(2,1)} %param.12), kind=kOutput, calls=%fused_computation.17 | convolution fusion | flops 807403520 | bytes 5963776 | tf_op jit(solution)/shard_map/dot_general | solution.py:78
  12.8 0.0 reduce-scatter.2.cloned.1.call-update
  12.8 0.0 copy-start.3
  12.8 0.0 all-gather.5.cloned.1.call-start
  12.9 73.1 %all-gather.3.cloned.1.call-done = bf16[4096,512]{1,0:T(8,128)(2,1)} async-done(((bf16[256,512]{1,0:T(8,128)(2,1)}), bf16[4096,512]{1,0:T(8,128)(2,1)}) %all-gather.3.cloned.1.call-update) | async-done | bytes 4194320 | tf_op jit(solution)/shard_map/all_gather | solution.py:75
  86.0 0.0 copy-done.4
  86.0 4.8 %convolution_convert_fusion.1 = bf16[192,4096]{1,0:T(8,128)(2,1)} fusion(bf16[192,512]{1,0:T(8,128)(2,1)S(1)} %copy-done.4, bf16[4096,512]{1,0:T(8,128)(2,1)} %all-gather.3.cloned.1.call-done), kind=kOutput, calls=%fused_computation.18 | convolution fusion | flops 806092800 | bytes 5963776 | tf_op jit(solution)/shard_map/dot_general | solution.py:67
  90.9 77.3 %reduce-scatter.2.cloned.1.call-done = bf16[256,512]{1,0:T(8,128)(2,1)} async-done(((bf16[4096,512]{1,0:T(8,128)(2,1)}), bf16[256,512]{1,0:T(8,128)(2,1)}) %reduce-scatter.2.cloned.1.call-update) | async-done | bytes 262160 | tf_op jit(solution)/shard_map/reduce_scatter | solution.py:77
  168.2 0.0 copy-done.1
  168.2 3.6 %convolution_bitcast_fusion.1 = f32[1,256,512]{1,2,0:T(8,128)} fusion(bf16[256,512]{1,0:T(8,128)(2,1)} %reduce-scatter.2.cloned.1.call-done, f32[1,256,512]{2,1,0:T(8,128)S(1)} %copy-done.1, f32[256]{0:T(256)S(1)} %get-tuple-element.184, f32[256]{0:T(256)S(1)} %get-tuple-element.183), kind=kOutput, calls=%fused_computation.21 | convolution fusion | flops 403243008 | bytes 1312768 | tf_op jit(solution)/shard_map/kn,bnc->bkc/dot_general | solution.py:20
  171.8 1.2 copy.17
  173.1 2.1 while.33
  173.1 0.5 select_reduce_fusion.6
  173.6 0.5 select_reduce_fusion.6
  174.1 0.5 select_reduce_fusion.6
  174.7 0.5 select_reduce_fusion.6
  175.2 0.6 convert_bitcast_fusion
  175.8 0.0 all-gather.5.cloned.1.call-update
  175.8 0.0 copy-start.2
  175.8 3.1 %while.34 = (s32[]{:T(128)}, f32[1,256,512]{2,1,0:T(8,128)S(1)}, s32[4,1,8,512]{3,2,1,0:T(8,128)S(1)}, f32[4,1,8,512]{3,2,1,0:T(8,128)S(1)}, s32[]{:T(128)}, /*index=5*/s32[]{:T(128)}) while((s32[]{:T(128)}, f32[1,256,512]{2,1,0:T(8,128)S(1)}, s32[4,1,8,512]{3,2,1,0:T(8,128)S(1)}, f32[4,1,8,512]{3,2,1,0:T(8,128)S(1)}, s32[]{:T(128)}, ...), condition=%wide.region_6.7_spmd.clone, body=%wide.region_4.6_spmd.clone.sunk | while | flops 3276803 | bytes 2195543 | solution.py:62
  175.9 0.5 select_reduce_fusion.7
  176.4 0.2 bitcast_add_fusion.6
  176.6 0.5 select_reduce_fusion.7
  177.2 0.2 bitcast_add_fusion.6
  177.4 0.5 select_reduce_fusion.7
  177.9 0.2 bitcast_add_fusion.6
  178.2 0.5 select_reduce_fusion.7
  178.7 0.2 bitcast_add_fusion.6
  178.9 0.0 copy-done.2
  178.9 3.4 %fusion.6 = f32[1,256,512]{2,1,0:T(8,128)} fusion(f32[1,256,512]{2,1,0:T(8,128)S(1)} %get-tuple-element.85, bf16[256,512]{1,0:T(8,128)(2,1)S(1)} %copy-done.2, f32[1,256,512]{2,1,0:T(8,128)} %param.14, f32[256]{0:T(256)S(1)} %get-tuple-element.184, f32[256]{0:T(256)S(1)} %get-tuple-element.183), kind=kOutput, calls=%fused_computation.22 | convolution fusion | flops 403374080 | bytes 1837056 | tf_op jit(solution)/shard_map/kn,bkc->bnc/dot_general | solution.py:24
  182.4 84.1 %all-gather.5.cloned.1.call-done = bf16[32,1,32,512]{3,2,1,0:T(8,128)(2,1)} async-done(((bf16[1,1,32,512]{3,2,1,0:T(8,128)(2,1)}), bf16[32,1,32,512]{3,2,1,0:T(8,128)(2,1)}) %all-gather.5.cloned.1.call-update) | async-done | bytes 1048592 | tf_op jit(solution)/shard_map/all_gather | solution.py:94
  266.5 1.4 convert_reduce_fusion
  267.9 3.1 %while.35 = (s32[]{:T(128)}, f32[1,256,512]{2,1,0:T(8,128)S(1)}, s32[4,1,8,512]{3,2,1,0:T(8,128)S(1)}, f32[4,1,8,512]{3,2,1,0:T(8,128)S(1)}, s32[]{:T(128)}, /*index=5*/s32[]{:T(128)}) while((s32[]{:T(128)}, f32[1,256,512]{2,1,0:T(8,128)S(1)}, s32[4,1,8,512]{3,2,1,0:T(8,128)S(1)}, f32[4,1,8,512]{3,2,1,0:T(8,128)S(1)}, ...), condition=%wide.region_10.11_spmd.clone, body=%wide.region_8.10_spmd.clone.sunk | while | flops 3276803 | bytes 2195543 | solution.py:62
  267.9 0.5 select_reduce_fusion.8
  268.4 0.2 bitcast_add_fusion.7
  268.7 0.5 select_reduce_fusion.8
  269.2 0.2 bitcast_add_fusion.7
  269.5 0.5 select_reduce_fusion.8
  270.0 0.2 bitcast_add_fusion.7
  270.2 0.5 select_reduce_fusion.8
  270.8 0.2 bitcast_add_fusion.7
  271.0 1.8 fusion.7
  272.8 0.8 copy.19
  (32 shorter events, 0.2 us)
Async XLA Ops:
  7.2 1.4 copy-start
  7.2 78.8 %all-gather.3.cloned.1.call-start = ((), (), s32[]{:S(2)}) async-start(), calls=%async_computation.1 | async-start | bytes 4456448 | tf_op jit(solution)/shard_map/all_gather | solution.py:75
  7.9 160.3 %reduce-scatter.2.cloned.1.call-start = ((), (), s32[]{:S(2)}) async-start(), calls=%async_computation.2 | async-start | bytes 4456448 | tf_op jit(solution)/shard_map/reduce_scatter | solution.py:77
  12.8 73.3 %copy-start.4 = (bf16[192,512]{1,0:T(8,128)(2,1)S(1)}, bf16[192,512]{1,0:T(8,128)(2,1)}, u32[]{:S(2)}) copy-start(bf16[192,512]{1,0:T(8,128)(2,1)} %param.12) | copy-start | bytes 589828
  12.8 155.4 %copy-start.1 = (f32[1,256,512]{2,1,0:T(8,128)S(1)}, f32[1,256,512]{2,1,0:T(8,128)}, u32[]{:S(2)}) copy-start(f32[1,256,512]{2,1,0:T(8,128)} %param.14) | copy-start | bytes 1572868
  12.8 160.3 %copy-start.3 = (s32[1,32,512]{2,1,0:T(8,128)S(1)}, s32[1,32,512]{2,1,0:T(8,128)}, u32[]{:S(2)}) copy-start(s32[1,32,512]{2,1,0:T(8,128)} %param.15) | copy-start | bytes 196612
  12.8 253.6 %all-gather.5.cloned.1.call-start = ((), (), s32[]{:S(2)}) async-start(), calls=%async_computation.3 | async-start | bytes 1081344 | tf_op jit(solution)/shard_map/all_gather | solution.py:94
  175.8 3.1 %copy-start.2 = (bf16[256,512]{1,0:T(8,128)(2,1)S(1)}, bf16[256,512]{1,0:T(8,128)(2,1)}, u32[]{:S(2)}) copy-start(bf16[256,512]{1,0:T(8,128)(2,1)} %reduce-scatter.2.cloned.1.call-done) | copy-start | bytes 786436
Sparse Core Ops, SparseCore 0:
  10.1 75.8 all-gather.2
  88.9 79.2 reduce-scatter.1
  175.9 90.4 all-gather.4
where the time goes:
time: 281 us; the launch traced here: 280 us
  waiting for transfers between devices  235 us (84%)
  matrix products  17.9 us (6%)
  between operations  13.9 us (5%)
  other arithmetic  9.54 us (3%)
  local copies, waits for them, and re-layouts  2.94 us (1%)
    all_gather x1, waiting for transfers between devices, on_device(): lax.all_gather(bands[None], 'dp', axis=0, tiled=True).astype(jnp.float32)  84.1 us
    reduce_scatter x1, waiting for transfers between devices, on_device(): lax.psum_scatter(lax.dot_general(activations, cotangent, (((0,), (0,)), (...  77.3 us
    all_gather x1, waiting for transfers between devices, on_device(): lax.all_gather(weight, 'fsdp', axis=0, tiled=True)  73.1 us
  transfers between devices with their start and end apart: 3, of which 3 were waited for; matrix products, arithmetic and copies ran while one was open for 5% of the time, Pallas kernels for 0%

commit v1 on v0

--- a/solution.py
+++ b/solution.py
@@ -91,7 +91,10 @@
     bands = picked.astype(jnp.bfloat16)
     replicas = lax.axis_size("dp")
     summed = jnp.sum(
-        lax.all_gather(bands[None], "dp", axis=0, tiled=True).astype(jnp.float32), axis=0
+        jnp.concatenate(
+            lax.all_to_all(jnp.stack([bands[None]] * lax.axis_size("dp")), "dp", 0, 0), axis=0
+        ).astype(jnp.float32),
+        axis=0,
     )
     mean_band = summed / replicas
     update = (

time: 281 us -> 239 us (0.85)
  waiting for transfers between devices: 235 us -> 173 us
  starting transfers between devices: 0.12 us -> 20.3 us
    all_gather x1 -> x0, waiting for transfers between devices: 84.1 us -> none  [on_device(): lax.all_gather(bands[None], 'dp', axis=0, tiled=True).astype(jnp.float32)]
    all_to_all x0 -> x1, waiting for transfers between devices: none -> 21.6 us  [on_device(): lax.all_to_all(jnp.stack([bands[None]] * lax.axis_size('dp')), 'dp', 0, 0)]
    all_to_all x0 -> x1, starting transfers between devices: none -> 20.2 us  [on_device(): lax.all_to_all(jnp.stack([bands[None]] * lax.axis_size('dp')), 'dp', 0, 0)]
  transfers between devices with their start and end apart: 3 -> 3, of which waited for: 3 -> 3; matrix products, arithmetic and copies ran while one was open for 5% -> 6% of each run, Pallas kernels for 0% -> 0%
where the time goes in v1:
time: 239 us
  waiting for transfers between devices  173 us (72%)
  starting transfers between devices  20.3 us (8%)
  matrix products  17.9 us (7%)
  between operations  14.2 us (6%)
  other arithmetic  8.93 us (4%)
  local copies, waits for them, and re-layouts  4.08 us (2%)
    reduce_scatter x1, waiting for transfers between devices, on_device(): lax.psum_scatter(lax.dot_general(activations, cotangent, (((0,), (0,)), (...  77.3 us
    all_gather x1, waiting for transfers between devices, on_device(): lax.all_gather(weight, 'fsdp', axis=0, tiled=True)  73.2 us
    all_to_all x1, waiting for transfers between devices, on_device(): lax.all_to_all(jnp.stack([bands[None]] * lax.axis_size('dp')), 'dp', 0, 0)  21.6 us
    all_to_all x1, starting transfers between devices, on_device(): lax.all_to_all(jnp.stack([bands[None]] * lax.axis_size('dp')), 'dp', 0, 0)  20.2 us
    dot_general x2, matrix products, inverse_blocks(): jnp.einsum('kn,bkc->bnc', table, coeffs, precision=lax.Precision.HIGHEST)  5.26 us
    dot_general x1, matrix products, contract_last(): lax.dot_general(left, right, (((1,), (1,)), ((), ())), preferred_element_...  4.84 us
  transfers between devices with their start and end apart: 3, of which 3 were waited for; matrix products, arithmetic and copies ran while one was open for 6% of the time, Pallas kernels for 0%

profile of v1, /device:TPU:1, one launch (start us, length us, event | category | flops | bytes accessed | tf_op | source)
XLA Modules:
  0.0 238.7 jit_solution(5416888851404773736)
XLA Ops:
  7.2 0.0 copy-start
  7.2 0.0 all-gather.2.cloned.1.call-start
  7.2 0.7 all-gather.2.cloned.1.call-update
  7.9 0.0 reduce-scatter.2.cloned.1.call-start
  8.0 0.6 copy-done
  8.6 4.2 %convolution_convert_fusion = bf16[4096,512]{1,0:T(8,128)(2,1)} fusion(bf16[192,4096]{1,0:T(8,128)(2,1)S(1)} %copy-done, bf16[192,512]{1,0:T(8,128)(2,1)} %param.12), kind=kOutput, calls=%fused_computation.17 | convolution fusion | flops 807403520 | bytes 5963776 | tf_op jit(solution)/shard_map/dot_general | solution.py:78
  12.8 0.0 reduce-scatter.2.cloned.1.call-update
  12.8 0.0 copy-start.3
  12.9 73.2 %all-gather.2.cloned.1.call-done = bf16[4096,512]{1,0:T(8,128)(2,1)} async-done(((bf16[256,512]{1,0:T(8,128)(2,1)}), bf16[4096,512]{1,0:T(8,128)(2,1)}) %all-gather.2.cloned.1.call-update) | async-done | bytes 4194320 | tf_op jit(solution)/shard_map/all_gather | solution.py:75
  86.0 0.0 copy-done.4
  86.0 4.8 %convolution_convert_fusion.1 = bf16[192,4096]{1,0:T(8,128)(2,1)} fusion(bf16[192,512]{1,0:T(8,128)(2,1)S(1)} %copy-done.4, bf16[4096,512]{1,0:T(8,128)(2,1)} %all-gather.2.cloned.1.call-done), kind=kOutput, calls=%fused_computation.18 | convolution fusion | flops 806092800 | bytes 5963776 | tf_op jit(solution)/shard_map/dot_general | solution.py:67
  90.9 77.3 %reduce-scatter.2.cloned.1.call-done = bf16[256,512]{1,0:T(8,128)(2,1)} async-done(((bf16[4096,512]{1,0:T(8,128)(2,1)}), bf16[256,512]{1,0:T(8,128)(2,1)}) %reduce-scatter.2.cloned.1.call-update) | async-done | bytes 262160 | tf_op jit(solution)/shard_map/reduce_scatter | solution.py:77
  168.2 0.0 copy-done.1
  168.2 3.6 %convolution_bitcast_fusion.1 = f32[1,256,512]{1,2,0:T(8,128)} fusion(bf16[256,512]{1,0:T(8,128)(2,1)} %reduce-scatter.2.cloned.1.call-done, f32[1,256,512]{2,1,0:T(8,128)S(1)} %copy-done.1, f32[256]{0:T(256)S(1)} %get-tuple-element.181, f32[256]{0:T(256)S(1)} %get-tuple-element.180), kind=kOutput, calls=%fused_computation.21 | convolution fusion | flops 403243008 | bytes 1312768 | tf_op jit(solution)/shard_map/kn,bnc->bkc/dot_general | solution.py:20
  171.8 1.2 copy.14
  173.1 0.0 copy-done.3
  173.1 2.1 while.33
  173.1 0.5 select_reduce_fusion.6
  173.6 0.5 select_reduce_fusion.6
  174.1 0.5 select_reduce_fusion.6
  174.7 0.5 select_reduce_fusion.6
  175.2 1.1 stack.3
  176.3 20.2 %all-to-all-start = ((bf16[32,1,1,32,512]{4,3,2,1,0:T(8,128)(2,1)}), bf16[32,1,1,32,512]{4,3,2,1,0:T(8,128)(2,1)}, u32[]{:S(2)}, u32[]{:S(2)}) async-start(bf16[32,1,1,32,512]{4,3,2,1,0:T(8,128)(2,1)} %stack.3), calls=%async_computation.1 | async-start | bytes 2097152 | tf_op jit(solution)/shard_map/all_to_all | solution.py:95
  196.5 0.0 copy-start.2
  196.6 3.1 %while.34 = (s32[]{:T(128)}, f32[1,256,512]{2,1,0:T(8,128)S(1)}, s32[4,1,8,512]{3,2,1,0:T(8,128)S(1)}, f32[4,1,8,512]{3,2,1,0:T(8,128)S(1)}, s32[]{:T(128)}, /*index=5*/s32[]{:T(128)}) while((s32[]{:T(128)}, f32[1,256,512]{2,1,0:T(8,128)S(1)}, s32[4,1,8,512]{3,2,1,0:T(8,128)S(1)}, f32[4,1,8,512]{3,2,1,0:T(8,128)S(1)}, s32[]{:T(128)}, ...), condition=%wide.region_6.7_spmd.clone, body=%wide.region_4.6_spmd.clone.sunk | while | flops 3276803 | bytes 2195543 | solution.py:62
  196.6 0.5 select_reduce_fusion.7
  197.1 0.2 bitcast_add_fusion.6
  197.4 0.5 select_reduce_fusion.7
  197.9 0.2 bitcast_add_fusion.6
  198.1 0.5 select_reduce_fusion.7
  198.7 0.2 bitcast_add_fusion.6
  198.9 0.5 select_reduce_fusion.7
  199.5 0.2 bitcast_add_fusion.6
  199.7 0.0 copy-done.2
  199.7 3.4 %fusion.6 = f32[1,256,512]{2,1,0:T(8,128)} fusion(f32[1,256,512]{2,1,0:T(8,128)S(1)} %get-tuple-element.85, bf16[256,512]{1,0:T(8,128)(2,1)S(1)} %copy-done.2, f32[1,256,512]{2,1,0:T(8,128)} %param.14, f32[256]{0:T(256)S(1)} %get-tuple-element.181, f32[256]{0:T(256)S(1)} %get-tuple-element.180), kind=kOutput, calls=%fused_computation.22 | convolution fusion | flops 403374080 | bytes 1837056 | tf_op jit(solution)/shard_map/kn,bkc->bnc/dot_general | solution.py:24
  203.1 21.6 %all-to-all-done = bf16[32,1,1,32,512]{4,3,2,1,0:T(8,128)(2,1)} async-done(((bf16[32,1,1,32,512]{4,3,2,1,0:T(8,128)(2,1)}), bf16[32,1,1,32,512]{4,3,2,1,0:T(8,128)(2,1)}, u32[]{:S(2)}, u32[]{:S(2)}) %all-to-all-start) | async-done | bytes 1048608 | tf_op jit(solution)/shard_map/all_to_all | solution.py:95
  224.7 1.4 convert_reduce_fusion
  226.1 3.1 %while.35 = (s32[]{:T(128)}, f32[1,256,512]{2,1,0:T(8,128)S(1)}, s32[4,1,8,512]{3,2,1,0:T(8,128)S(1)}, f32[4,1,8,512]{3,2,1,0:T(8,128)S(1)}, s32[]{:T(128)}, /*index=5*/s32[]{:T(128)}) while((s32[]{:T(128)}, f32[1,256,512]{2,1,0:T(8,128)S(1)}, s32[4,1,8,512]{3,2,1,0:T(8,128)S(1)}, f32[4,1,8,512]{3,2,1,0:T(8,128)S(1)}, ...), condition=%wide.region_10.11_spmd.clone, body=%wide.region_8.10_spmd.clone.sunk | while | flops 3276803 | bytes 2195543 | solution.py:62
  226.2 0.5 select_reduce_fusion.8
  226.7 0.2 bitcast_add_fusion.7
  226.9 0.5 select_reduce_fusion.8
  227.5 0.2 bitcast_add_fusion.7
  227.7 0.5 select_reduce_fusion.8
  228.3 0.2 bitcast_add_fusion.7
  228.5 0.5 select_reduce_fusion.8
  229.0 0.2 bitcast_add_fusion.7
  229.2 1.8 fusion.7
  231.1 0.8 copy.17
  (32 shorter events, 0.2 us)
Async XLA Ops:
  7.2 1.4 copy-start
  7.2 78.8 %all-gather.2.cloned.1.call-start = ((), (), s32[]{:S(2)}) async-start(), calls=%async_computation.2 | async-start | bytes 4456448 | tf_op jit(solution)/shard_map/all_gather | solution.py:75
  7.9 160.3 %reduce-scatter.2.cloned.1.call-start = ((), (), s32[]{:S(2)}) async-start(), calls=%async_computation.3 | async-start | bytes 4456448 | tf_op jit(solution)/shard_map/reduce_scatter | solution.py:77
  12.8 73.2 %copy-start.4 = (bf16[192,512]{1,0:T(8,128)(2,1)S(1)}, bf16[192,512]{1,0:T(8,128)(2,1)}, u32[]{:S(2)}) copy-start(bf16[192,512]{1,0:T(8,128)(2,1)} %param.12) | copy-start | bytes 589828
  12.8 155.4 %copy-start.1 = (f32[1,256,512]{2,1,0:T(8,128)S(1)}, f32[1,256,512]{2,1,0:T(8,128)}, u32[]{:S(2)}) copy-start(f32[1,256,512]{2,1,0:T(8,128)} %param.14) | copy-start | bytes 1572868
  12.8 160.3 %copy-start.3 = (s32[1,32,512]{2,1,0:T(8,128)S(1)}, s32[1,32,512]{2,1,0:T(8,128)}, u32[]{:S(2)}) copy-start(s32[1,32,512]{2,1,0:T(8,128)} %param.15) | copy-start | bytes 196612
  176.3 48.4 %all-to-all-start = ((bf16[32,1,1,32,512]{4,3,2,1,0:T(8,128)(2,1)}), bf16[32,1,1,32,512]{4,3,2,1,0:T(8,128)(2,1)}, u32[]{:S(2)}, u32[]{:S(2)}) async-start(bf16[32,1,1,32,512]{4,3,2,1,0:T(8,128)(2,1)} %stack.3), calls=%async_computation.1 | async-start | bytes 2097152 | tf_op jit(solution)/shard_map/all_to_all | solution.py:95
  196.5 3.1 %copy-start.2 = (bf16[256,512]{1,0:T(8,128)(2,1)S(1)}, bf16[256,512]{1,0:T(8,128)(2,1)}, u32[]{:S(2)}) copy-start(bf16[256,512]{1,0:T(8,128)(2,1)} %reduce-scatter.2.cloned.1.call-done) | copy-start | bytes 786436
Sparse Core Ops, SparseCore 0:
  10.1 75.8 all-gather.1
  88.9 79.2 reduce-scatter.1
